TPU v7x, 32 devices: a whole 2x2x4 slice. The times are simulated.
32 devices in a mesh: dp: 16 (over z, y, x), tensor: 2 (over core).
Axes of the slice: x: 2, y: 2, z: 4, core: 2. Of those that a mesh axis runs over, the one named last changes fastest.
Arguments:
- hidden: bfloat16 [128, 4096], P('dp'), may hold values from -20 to 20
- gain: bfloat16 [4096], replicated, may hold values from 0.5 to 1.5
- head: bfloat16 [4096, 4096], P(('dp', 'tensor')), may hold values from -32 to 32
- moment: bfloat16 [4096, 4096], P(('dp', 'tensor')), may hold values from -6 to 6
- second: float32 [4096], P(('dp', 'tensor')), may hold values from 0.5 to 50
- labels: int32 [128], P('dp'), may hold values from 0 to 4095
Outputs:
- grad_hidden: bfloat16 [128, 4096], P('dp')
- grad_gain: float32 [4096], replicated
- head_new: bfloat16 [4096, 4096], P(('dp', 'tensor'))
- moment_new: bfloat16 [4096, 4096], P(('dp', 'tensor'))
- second_new: float32 [4096], P(('dp', 'tensor'))
All inputs are finite; a program needn't handle non-finite values.
Results may differ from a plain program's by a relative error of at most 0.01.
Values may be sent and summed in bfloat16 or wider, within the bound.
A program may use at most 64 MiB of HBM per device.

v0:
```python
import jax
import jax.numpy as jnp
from jax import lax
from jax.sharding import PartitionSpec as P

D = 4096
loss_scale = 16.0
beta_one = 0.9
beta_two = 0.999
adam_eps = 1e-08
step_size = 0.02
norm_eps = 1e-05
bias_one = 1.0 - 0.9**10
bias_two = 1.0 - 0.999**10


def inverse_norm(values_f):
    squares = jnp.sum(values_f * values_f, axis=1)
    return lax.rsqrt(squares / D + norm_eps)


def softmax_grad(logits, targets, vocab_ids):
    local_max = jnp.max(logits, axis=1)
    local_sum = jnp.sum(jnp.exp(logits - local_max[:, None]), axis=1)
    global_max = lax.pmax(local_max, ("dp", "tensor"))
    global_sum = lax.psum(local_sum * jnp.exp(local_max - global_max), ("dp", "tensor"))
    onehot = (targets[:, None] == vocab_ids[None, :]).astype(jnp.float32)
    probability = jnp.exp(logits - global_max[:, None]) / global_sum[:, None]
    return (loss_scale * (probability - onehot)).astype(jnp.bfloat16)


def norm_backward(grad_normed, hidden_part, rstd_part, gain_f):
    inner_sums = jnp.sum(grad_normed * gain_f * hidden_part, axis=1)
    return (
        rstd_part[:, None] * gain_f * grad_normed
        - hidden_part * (rstd_part**3)[:, None] * inner_sums[:, None] / D
    ).astype(jnp.bfloat16)


def local(hidden, gain, head, moment, second, labels):
    hidden_f = hidden.astype(jnp.float32)
    gain_f = gain.astype(jnp.float32)
    rstd = inverse_norm(hidden_f)
    normed = (hidden_f * rstd[:, None] * gain_f).astype(jnp.bfloat16)
    normed_all = lax.all_gather(normed, "dp", axis=0, tiled=True)
    all_labels = lax.all_gather(labels, "dp", axis=0, tiled=True)
    own_rows = head.shape[0]
    tensor_count = lax.axis_size("tensor")
    dp_count = lax.axis_size("dp")
    owner = lax.axis_index("dp") * tensor_count + lax.axis_index("tensor")
    vocab_ids = owner * own_rows + jnp.arange(own_rows, dtype=jnp.int32)
    logits = lax.dot_general(
        normed_all, head, (((1,), (1,)), ((), ())), preferred_element_type=jnp.float32
    )
    dlogits = softmax_grad(logits, all_labels, vocab_ids)
    grad_head = lax.dot_general(
        dlogits, normed_all, (((0,), (0,)), ((), ())), preferred_element_type=jnp.float32
    )
    share_rows = hidden.shape[0] // tensor_count
    ordered = dlogits.reshape(dp_count, tensor_count, share_rows, own_rows).transpose(1, 0, 2, 3)
    ordered = ordered.reshape(tensor_count * dp_count * share_rows, own_rows)
    tensor_sum = lax.psum_scatter(
        jnp.dot(ordered, head, preferred_element_type=jnp.float32).astype(jnp.bfloat16),
        "tensor",
        scatter_dimension=0,
        tiled=True,
    ).astype(jnp.float32)
    full_sum = lax.psum(tensor_sum, "dp")
    grad_normed = lax.dynamic_slice_in_dim(
        full_sum, lax.axis_index("dp") * share_rows, share_rows, 0
    )
    offset = lax.axis_index("tensor") * share_rows
    hidden_part = lax.dynamic_slice_in_dim(hidden_f, offset, share_rows, 0)
    rstd_part = lax.dynamic_slice_in_dim(rstd, offset, share_rows, 0)
    grad_gain = lax.psum(
        jnp.sum(grad_normed * hidden_part * rstd_part[:, None], axis=0), ("dp", "tensor")
    )
    part_grad = norm_backward(grad_normed, hidden_part, rstd_part, gain_f)
    grad_hidden = lax.all_gather(part_grad, "tensor", axis=0, tiled=True)
    row_sums = jnp.sum(grad_head * grad_head, axis=1)
    second_new = beta_two * second + (1.0 - beta_two) * row_sums / D
    first = beta_one * moment.astype(jnp.float32) + (1.0 - beta_one) * grad_head
    adam_step = first / bias_one / (jnp.sqrt(second_new / bias_two)[:, None] + adam_eps)
    head_new = (head.astype(jnp.float32) - step_size * adam_step).astype(jnp.bfloat16)
    return (grad_hidden, grad_gain, head_new, first.astype(jnp.bfloat16), second_new)


def solution(mesh):
    placed = (
        P("dp", None),
        P(),
        P(("dp", "tensor"), None),
        P(("dp", "tensor"), None),
        P(("dp", "tensor")),
        P("dp"),
    )
    return jax.shard_map(
        local,
        mesh=mesh,
        in_specs=placed,
        out_specs=(
            P("dp", None),
            P(),
            P(("dp", "tensor"), None),
            P(("dp", "tensor"), None),
            P(("dp", "tensor")),
        ),
        check_vma=False,
    )
```

profile of v0, /device:TPU:12, one launch (start us, length us, event | category | flops | bytes accessed | tf_op | source)
XLA Modules:
  0.0 299.2 jit_solution(8603135255991691037)
XLA Ops:
  7.2 0.0 copy-start
  7.2 0.0 all-gather.3.cloned.1.call-start
  7.2 0.8 convert_element_type.37
  8.0 1.0 multiply_reduce_fusion.1
  9.0 1.6 multiply_convert_fusion
  10.6 0.0 all-gather.3.cloned.1.call-update
  10.6 0.0 reduce-scatter.2.cloned.1.call-start
  10.6 1.2 dynamic-slice
  12.5 0.9 dynamic-update-slice
  13.4 12.6 %all-reduce = s32[128]{0:T(128)S(1)} all-reduce(s32[128]{0:T(128)S(1)} %dynamic-update-slice), channel_id=1, replica_groups=mesh['dp'=16,'tensor'=2] {'dp'}, use_global_device_ids=true, to_apply=%add | all-reduce | flops 128 | bytes 1024
  26.0 40.8 %all-gather.3.cloned.1.call-done = bf16[128,4096]{1,0:T(8,128)(2,1)} async-done(((bf16[8,4096]{1,0:T(8,128)(2,1)}), bf16[128,4096]{1,0:T(8,128)(2,1)}) %all-gather.3.cloned.1.call-update) | async-done | bytes 1048592 | tf_op jit(solution)/shard_map/all_gather | solution.py:45
  66.8 2.1 fusion.2
  68.9 0.0 copy-start.3
  68.9 40.0 %pmax.7 = f32[128]{0:T(128)S(1)} all-reduce(f32[128]{0:T(128)S(1)} %get-tuple-element.13), channel_id=1, replica_groups=mesh['dp'=16,'tensor'=2] {'dp','tensor'}, use_global_device_ids=true, to_apply=%region_2.0 | all-reduce | flops 128 | bytes 1024 | tf_op jit(solution)/shard_map/pmax | solution.py:25
  108.9 0.2 exponential_reduce_fusion
  109.1 40.0 %psum.21 = f32[128]{0:T(128)S(1)} all-reduce(f32[128]{0:T(128)S(1)} %exponential_multiply_fusion), channel_id=1, replica_groups=mesh['dp'=16,'tensor'=2] {'dp','tensor'}, use_global_device_ids=true, to_apply=%region_4.0 | all-reduce | flops 128 | bytes 1024 | tf_op jit(solution)/shard_map/psum | solution.py:26
  149.1 0.1 multiply_convert_fusion.1
  149.3 1.5 convolution_convert_fusion
  150.7 0.0 reduce-scatter.2.cloned.1.call-update
  150.8 0.0 copy-done.3
  150.8 0.1 multiply_multiply_fusion
  150.9 0.5 multiply_reduce_fusion
  151.4 0.5 sqrt_add_fusion
  152.0 0.0 copy-done.2
  152.0 2.1 fusion
  154.1 5.4 %reduce-scatter.2.cloned.1.call-done = bf16[64,4096]{1,0:T(8,128)(2,1)} async-done(((bf16[128,4096]{1,0:T(8,128)(2,1)}), bf16[64,4096]{1,0:T(8,128)(2,1)}) %reduce-scatter.2.cloned.1.call-update) | async-done | bytes 524304 | tf_op jit(solution)/shard_map/reduce_scatter | solution.py:62
  159.5 81.5 %all-reduce.2 = f32[64,4096]{1,0:T(8,128)S(1)} all-reduce(bf16[64,4096]{1,0:T(8,128)(2,1)} %reduce-scatter.2.cloned.1.call-done), channel_id=1, replica_groups=mesh['dp'=16,'tensor'=2] {'dp'}, use_global_device_ids=true, to_apply=%region_6.0 | all-reduce | flops 262144 | bytes 1572864 | tf_op jit(solution)/shard_map/psum | solution.py:68
  241.0 0.2 multiply_reduce_fusion.2
  241.2 0.1 fusion.1
  241.3 1.9 all-gather
  243.1 0.7 reshape.41
  243.8 48.6 %psum.23 = f32[4096]{0:T(1024)} all-reduce(f32[4096]{0:T(1024)S(1)} %get-tuple-element.5), channel_id=1, replica_groups=mesh['dp'=16,'tensor'=2] {'dp','tensor'}, use_global_device_ids=true, to_apply=%region_9.0 | all-reduce | flops 4096 | bytes 32768 | tf_op jit(solution)/shard_map/psum | solution.py:75
  (12 shorter events, 0.1 us)
Async XLA Ops:
  7.2 142.1 %copy-start = (bf16[128,4096]{1,0:T(8,128)(2,1)S(1)}, bf16[128,4096]{1,0:T(8,128)(2,1)}, u32[]{:S(2)}) copy-start(bf16[128,4096]{1,0:T(8,128)(2,1)} %param.8) | copy-start | bytes 3145732
  7.2 59.6 %all-gather.3.cloned.1.call-start = ((), (), s32[]{:S(2)}) async-start(), calls=%async_computation.1 | async-start | bytes 1114112 | tf_op jit(solution)/shard_map/all_gather | solution.py:45
  10.6 148.9 %reduce-scatter.2.cloned.1.call-start = ((), (), s32[]{:S(2)}) async-start(), calls=%async_computation.2 | async-start | bytes 1572864 | tf_op jit(solution)/shard_map/reduce_scatter | solution.py:62
  68.9 81.9 %copy-start.3 = (bf16[8,4096]{1,0:T(8,128)(2,1)S(1)}, bf16[8,4096]{1,0:T(8,128)(2,1)}, u32[]{:S(2)}) copy-start(bf16[8,4096]{1,0:T(8,128)(2,1)} %param.6) | copy-start | bytes 196612
  68.9 82.0 %copy-start.1 = (bf16[128,4096]{1,0:T(8,128)(2,1)S(1)}, bf16[128,4096]{1,0:T(8,128)(2,1)}, u32[]{:S(2)}) copy-start(bf16[128,4096]{1,0:T(8,128)(2,1)} %all-gather.3.cloned.1.call-done) | copy-start | bytes 3145732
  150.7 0.7 copy-start.4
  150.7 1.2 copy-start.2
Sparse Core Ops, SparseCore 0:
  11.3 55.4 all-gather.2
  150.9 8.5 reduce-scatter.1
where the time goes:
time: 300 us; the launch traced here: 299 us
  blocking collectives  225 us (75%)
  waiting for transfers between devices  46.2 us (15%)
  between operations  14.8 us (5%)
  other arithmetic  6.64 us (2%)
  matrix products  4.05 us (1%)
    psum x1, blocking collectives, local(): full_sum = lax.psum(tensor_sum, 'dp')  81.5 us
    psum x1, blocking collectives, local(): lax.psum(jnp.sum(grad_normed * hidden_part * rstd_part[:, None], axis=0),...  48.6 us
    all_gather x1, waiting for transfers between devices, local(): normed_all = lax.all_gather(normed, 'dp', axis=0, tiled=True)  40.8 us
    pmax x1, blocking collectives, softmax_grad(): global_max = lax.pmax(local_max, ('dp', 'tensor'))  40 us
    psum x1, blocking collectives, softmax_grad(): lax.psum(local_sum * jnp.exp(local_max - global_max), ('dp', 'tensor'))  40 us
    unnamed x1, blocking collectives  12.6 us
  transfers between devices with their start and end apart: 2, of which 2 were waited for; matrix products, arithmetic and copies ran while one was open for 2% of the time, Pallas kernels for 0%

commit v1 on v0

--- a/solution.py
+++ b/solution.py
@@ -12,6 +12,16 @@
 norm_eps = 1e-05
 bias_one = 1.0 - 0.9**10
 bias_two = 1.0 - 0.999**10
+
+
+def supply_all_map(frame_in):
+    total_devices = lax.axis_size("dp")
+    formed = frame_in
+    for s in [hop_no for hop_no in (1, 2, 4, 8, 16) if hop_no < total_devices]:
+        formed = formed + lax.ppermute(
+            formed, axis_name="dp", perm=[(at, at ^ s) for at in range(total_devices)]
+        )
+    return formed
 
 
 def inverse_norm(values_f):
@@ -65,7 +75,7 @@
         scatter_dimension=0,
         tiled=True,
     ).astype(jnp.float32)
-    full_sum = lax.psum(tensor_sum, "dp")
+    full_sum = supply_all_map(tensor_sum)
     grad_normed = lax.dynamic_slice_in_dim(
         full_sum, lax.axis_index("dp") * share_rows, share_rows, 0
     )

time: 300 us -> 335 us (1.12)
  waiting for transfers between devices: 46.2 us -> 160 us
  blocking collectives: 225 us -> 137 us
  starting transfers between devices: 0.08 us -> 5.25 us
  other arithmetic: 6.64 us -> 10.3 us
    ppermute x0 -> x4, waiting for transfers between devices: none -> 111 us  [supply_all_map(): lax.ppermute(formed, axis_name='dp', perm=[(at, at ^ s) for at in range(t...]
    psum x1 -> x0, blocking collectives: 81.5 us -> none  [local(): full_sum = lax.psum(tensor_sum, 'dp')]
    psum x1, blocking collectives: 48.6 us -> 42.6 us  [local(): lax.psum(jnp.sum(grad_normed * hidden_part * rstd_part[:, None], axis=0),...]
    ppermute x0 -> x4, starting transfers between devices: none -> 5.17 us  [supply_all_map(): lax.ppermute(formed, axis_name='dp', perm=[(at, at ^ s) for at in range(t...]
  transfers between devices with their start and end apart: 2 -> 6, of which waited for: 2 -> 6; matrix products, arithmetic and copies ran while one was open for 2% -> 2% of each run, Pallas kernels for 0% -> 0%
where the time goes in v1:
time: 335 us; the launch traced here: 334 us
  waiting for transfers between devices  160 us (48%)
  blocking collectives  137 us (41%)
  between operations  14.8 us (4%)
  other arithmetic  10.3 us (3%)
  starting transfers between devices  5.25 us (2%)
  matrix products  3.99 us (1%)
    ppermute x4, waiting for transfers between devices, supply_all_map(): lax.ppermute(formed, axis_name='dp', perm=[(at, at ^ s) for at in range(t...  111 us
    psum x1, blocking collectives, local(): lax.psum(jnp.sum(grad_normed * hidden_part * rstd_part[:, None], axis=0),...  42.6 us
    all_gather x1, waiting for transfers between devices, local(): normed_all = lax.all_gather(normed, 'dp', axis=0, tiled=True)  40.8 us
    pmax x1, blocking collectives, softmax_grad(): global_max = lax.pmax(local_max, ('dp', 'tensor'))  40 us
    psum x1, blocking collectives, softmax_grad(): lax.psum(local_sum * jnp.exp(local_max - global_max), ('dp', 'tensor'))  40 us
    unnamed x1, blocking collectives  12.6 us
    reduce_scatter x1, waiting for transfers between devices, local(): lax.psum_scatter(jnp.dot(ordered, head, preferred_element_type=jnp.float3...  8.69 us
  transfers between devices with their start and end apart: 6, of which 6 were waited for; matrix products, arithmetic and copies ran while one was open for 2% of the time, Pallas kernels for 0%

profile of v1, /device:TPU:12, one launch (start us, length us, event | category | flops | bytes accessed | tf_op | source)
XLA Modules:
  0.0 334.5 jit_solution(3166009098841074514)
XLA Ops:
  7.2 0.8 convert_element_type.37
  8.0 1.0 multiply_reduce_fusion.1
  9.0 1.6 multiply_convert_fusion
  10.6 1.2 dynamic-slice
  12.5 0.9 dynamic-update-slice
  13.4 12.6 %all-reduce = s32[128]{0:T(128)S(1)} all-reduce(s32[128]{0:T(128)S(1)} %dynamic-update-slice), channel_id=1, replica_groups=mesh['dp'=16,'tensor'=2] {'dp'}, use_global_device_ids=true, to_apply=%add | all-reduce | flops 128 | bytes 1024
  26.0 40.8 %all-gather.3.cloned.1.call-done = bf16[128,4096]{1,0:T(8,128)(2,1)} async-done(((bf16[8,4096]{1,0:T(8,128)(2,1)}), bf16[128,4096]{1,0:T(8,128)(2,1)}) %all-gather.3.cloned.1.call-update) | async-done | bytes 1048592 | tf_op jit(solution)/shard_map/all_gather | solution.py:55
  66.8 2.1 fusion.2
  68.9 40.0 %pmax.7 = f32[128]{0:T(128)S(1)} all-reduce(f32[128]{0:T(128)S(1)} %get-tuple-element.14), channel_id=1, replica_groups=mesh['dp'=16,'tensor'=2] {'dp','tensor'}, use_global_device_ids=true, to_apply=%region_2.0 | all-reduce | flops 128 | bytes 1024 | tf_op jit(solution)/shard_map/pmax | solution.py:35
  108.9 0.2 exponential_reduce_fusion
  109.1 40.0 %psum.14 = f32[128]{0:T(128)S(1)} all-reduce(f32[128]{0:T(128)S(1)} %exponential_multiply_fusion), channel_id=1, replica_groups=mesh['dp'=16,'tensor'=2] {'dp','tensor'}, use_global_device_ids=true, to_apply=%region_4.0 | all-reduce | flops 128 | bytes 1024 | tf_op jit(solution)/shard_map/psum | solution.py:36
  149.1 0.1 multiply_convert_fusion.1
  149.3 1.4 convolution_convert_fusion
  150.7 8.7 %reduce-scatter.2.cloned.1.call-done = bf16[64,4096]{1,0:T(8,128)(2,1)} async-done(((bf16[128,4096]{1,0:T(8,128)(2,1)}), bf16[64,4096]{1,0:T(8,128)(2,1)}) %reduce-scatter.2.cloned.1.call-update) | async-done | bytes 524304 | tf_op jit(solution)/shard_map/reduce_scatter | solution.py:72
  159.4 1.1 convert_element_type.42
  160.5 1.5 collective-permute-start
  162.0 23.9 %collective-permute-done = f32[64,4096]{1,0:T(8,128)S(1)} collective-permute-done((f32[64,4096]{1,0:T(8,128)S(1)}, f32[64,4096]{1,0:T(8,128)S(1)}, u32[]{:S(2)}, u32[]{:S(2)}) %collective-permute-start) | collective-permute-done | bytes 1048608 | tf_op jit(solution)/shard_map/ppermute | solution.py:21
  186.0 1.1 convert_add_fusion
  187.1 0.6 collective-permute-start.1
  187.7 24.1 %collective-permute-done.1 = f32[64,4096]{1,0:T(8,128)S(1)} collective-permute-done((f32[64,4096]{1,0:T(8,128)S(1)}, f32[64,4096]{1,0:T(8,128)S(1)}, u32[]{:S(2)}, u32[]{:S(2)}) %collective-permute-start.1) | collective-permute-done | bytes 1048608 | tf_op jit(solution)/shard_map/ppermute | solution.py:21
  211.9 0.6 collective-permute-start.2
  212.6 0.5 multiply_reduce_fusion
  213.1 0.5 sqrt_add_fusion
  213.6 22.1 %collective-permute-done.2 = f32[64,4096]{1,0:T(8,128)} collective-permute-done((f32[64,4096]{1,0:T(8,128)S(1)}, f32[64,4096]{1,0:T(8,128)}, u32[]{:S(2)}, u32[]{:S(2)}) %collective-permute-start.2) | collective-permute-done | bytes 1048608 | tf_op jit(solution)/shard_map/ppermute | solution.py:21
  235.8 1.3 add.65
  237.1 2.5 collective-permute-start.3
  239.6 2.1 fusion
  241.6 40.5 %collective-permute-done.3 = f32[64,4096]{1,0:T(8,128)S(1)} collective-permute-done((f32[64,4096]{1,0:T(8,128)S(1)}, f32[64,4096]{1,0:T(8,128)S(1)}, u32[]{:S(2)}, u32[]{:S(2)}) %collective-permute-start.3) | collective-permute-done | bytes 1048608 | tf_op jit(solution)/shard_map/ppermute | solution.py:21
  282.2 0.2 multiply_reduce_fusion.2
  282.5 1.9 all-gather
  284.3 0.7 reshape.41
  285.0 42.6 %psum.15 = f32[4096]{0:T(1024)} all-reduce(f32[4096]{0:T(1024)S(1)} %get-tuple-element.5), channel_id=1, replica_groups=mesh['dp'=16,'tensor'=2] {'dp','tensor'}, use_global_device_ids=true, to_apply=%region_8.0 | all-reduce | flops 4096 | bytes 32768 | tf_op jit(solution)/shard_map/psum | solution.py:85
  (23 shorter events, 0.5 us)
Async XLA Ops:
  7.2 142.1 %copy-start = (bf16[128,4096]{1,0:T(8,128)(2,1)S(1)}, bf16[128,4096]{1,0:T(8,128)(2,1)}, u32[]{:S(2)}) copy-start(bf16[128,4096]{1,0:T(8,128)(2,1)} %param.8) | copy-start | bytes 3145732
  7.2 59.6 %all-gather.3.cloned.1.call-start = ((), (), s32[]{:S(2)}) async-start(), calls=%async_computation.1 | async-start | bytes 1114112 | tf_op jit(solution)/shard_map/all_gather | solution.py:55
  10.6 148.8 %reduce-scatter.2.cloned.1.call-start = ((), (), s32[]{:S(2)}) async-start(), calls=%async_computation.2 | async-start | bytes 1572864 | tf_op jit(solution)/shard_map/reduce_scatter | solution.py:72
  160.5 25.5 %collective-permute-start = (f32[64,4096]{1,0:T(8,128)S(1)}, f32[64,4096]{1,0:T(8,128)S(1)}, u32[]{:S(2)}, u32[]{:S(2)}) collective-permute-start(f32[64,4096]{1,0:T(8,128)S(1)} %convert_element_type.42), channel_id=1, source_target_pairs={{0,2},{2,0},{4,6},{6,4},{8,10},{10,8},{12,14},{14,12},{16,18},{18,... | collective-permute-start | bytes 3145736 | tf_op jit(solution)/shard_map/ppermute | solution.py:21
  187.1 25.4 %copy-start.3 = (bf16[8,4096]{1,0:T(8,128)(2,1)S(1)}, bf16[8,4096]{1,0:T(8,128)(2,1)}, u32[]{:S(2)}) copy-start(bf16[8,4096]{1,0:T(8,128)(2,1)} %param.6) | copy-start | bytes 196612
  187.1 25.5 %copy-start.1 = (bf16[128,4096]{1,0:T(8,128)(2,1)S(1)}, bf16[128,4096]{1,0:T(8,128)(2,1)}, u32[]{:S(2)}) copy-start(bf16[128,4096]{1,0:T(8,128)(2,1)} %all-gather.3.cloned.1.call-done) | copy-start | bytes 3145732
  187.1 24.7 %collective-permute-start.1 = (f32[64,4096]{1,0:T(8,128)S(1)}, f32[64,4096]{1,0:T(8,128)S(1)}, u32[]{:S(2)}, u32[]{:S(2)}) collective-permute-start(f32[64,4096]{1,0:T(8,128)S(1)} %convert_add_fusion), channel_id=1, source_target_pairs={{0,4},{2,6},{4,0},{6,2},{8,12},{10,14},{12,8},{14,10},{16,20},{18,... | collective-permute-start | bytes 3145736 | tf_op jit(solution)/shard_map/ppermute | solution.py:21
  211.9 1.2 copy-start.4
  211.9 23.9 %collective-permute-start.2 = (f32[64,4096]{1,0:T(8,128)S(1)}, f32[64,4096]{1,0:T(8,128)}, u32[]{:S(2)}, u32[]{:S(2)}) collective-permute-start(f32[64,4096]{1,0:T(8,128)S(1)} %add.64), channel_id=1, source_target_pairs={{0,8},{2,10},{4,12},{6,14},{8,0},{10,2},{12,4},{14,6},{16,24},{18,... | collective-permute-start | bytes 3145736 | tf_op jit(solution)/shard_map/ppermute | solution.py:21
  213.1 26.5 %copy-start.2 = (bf16[128,4096]{1,0:T(8,128)(2,1)S(1)}, bf16[128,4096]{1,0:T(8,128)(2,1)}, u32[]{:S(2)}) copy-start(bf16[128,4096]{1,0:T(8,128)(2,1)} %param.9) | copy-start | bytes 3145732
  237.1 45.1 %collective-permute-start.3 = (f32[64,4096]{1,0:T(8,128)S(1)}, f32[64,4096]{1,0:T(8,128)S(1)}, u32[]{:S(2)}, u32[]{:S(2)}) collective-permute-start(f32[64,4096]{1,0:T(8,128)S(1)} %add.65), channel_id=1, source_target_pairs={{0,16},{2,18},{4,20},{6,22},{8,24},{10,26},{12,28},{14,30},{16,0},... | collective-permute-start | bytes 3145736 | tf_op jit(solution)/shard_map/ppermute | solution.py:21
Sparse Core Ops, SparseCore 0:
  11.3 55.4 all-gather.2
  150.8 8.5 reduce-scatter.1
